TPU v7x, 32 devices: a whole 2x2x4 slice. The times are simulated.
32 devices in a mesh: dp: 4 (over z), mp: 8 (over y, x, core).
Axes of the slice: x: 2, y: 2, z: 4, core: 2. Of those that a mesh axis runs over, the one named last changes fastest.
Arguments:
- tokens: bfloat16 [2048, 3072], P('dp', 'mp'), may hold values from -6 to 6
- w_first: bfloat16 [3072, 12288], P('dp', 'mp'), may hold values from -0.15625 to 0.15625
- w_second: bfloat16 [12288, 3072], P('mp', 'dp'), may hold values from -0.078125 to 0.078125
- cotangent: bfloat16 [2048, 3072], P('dp', 'mp'), may hold values from -1.5 to 1.5
Outputs:
- outputs: bfloat16 [2048, 3072], P('dp', 'mp')
- input_grad: bfloat16 [2048, 3072], P('dp', 'mp')
- first_grad: float32 [3072, 12288], P('dp', 'mp')
- second_grad: float32 [12288, 3072], P('mp', 'dp')
All inputs are finite; a program needn't handle non-finite values.
Results may differ from a plain program's by a relative error of at most 0.018.
Values may be sent and summed in bfloat16 or wider, within the bound.
No kernel may reach another device: no remote copies, remote signals or barrier semaphores. Data moves between devices by JAX's collectives and lax.ppermute only.
A program may use at most 128 MiB of HBM per device.

v0:
```python
import jax
import jax.numpy as jnp
from jax import lax
from jax.sharding import PartitionSpec as P

inv_root_two = 0.7071067811865476
inv_root_tau = 0.3989422804014327


def gelu_value(value):
    return 0.5 * value * (1.0 + lax.erf(value * inv_root_two))


def gelu_slope(value):
    return (
        0.5 * (1.0 + lax.erf(value * inv_root_two))
        + value * jnp.exp(-0.5 * value * value) * inv_root_tau
    )


def over_rows(left, right):
    return lax.dot_general(
        left, right, (((0,), (0,)), ((), ())), preferred_element_type=jnp.float32
    )


def over_columns(left, right):
    return lax.dot_general(
        left, right, (((1,), (1,)), ((), ())), preferred_element_type=jnp.float32
    )


def shards(tokens, w_first, w_second, cotangent):
    first_full = lax.all_gather(w_first, "dp", axis=0, tiled=True)
    second_full = lax.all_gather(w_second, "dp", axis=1, tiled=True)
    block = first_full
    pre_act = jnp.dot(
        lax.all_gather(tokens, "mp", axis=1, tiled=True), block, preferred_element_type=jnp.float32
    )
    activated = gelu_value(pre_act).astype(jnp.bfloat16)
    output_terms = jnp.dot(activated, second_full, preferred_element_type=jnp.float32)
    outputs = lax.psum_scatter(
        output_terms.astype(jnp.bfloat16), "mp", scatter_dimension=1, tiled=True
    )
    piece = lax.all_gather(cotangent, "mp", axis=1, tiled=True)
    block = second_full
    back_pre = over_columns(piece, block)
    hidden_grad = (back_pre * gelu_slope(pre_act)).astype(jnp.bfloat16)
    inputs_full = lax.all_gather(tokens, "mp", axis=1, tiled=True)
    second_terms = over_rows(activated, piece)
    second_grad = lax.psum_scatter(
        second_terms.astype(jnp.bfloat16), "dp", scatter_dimension=1, tiled=True
    ).astype(jnp.float32)
    first_terms = over_rows(inputs_full, hidden_grad)
    first_grad = lax.psum_scatter(
        first_terms.astype(jnp.bfloat16), "dp", scatter_dimension=0, tiled=True
    ).astype(jnp.float32)
    input_terms = over_columns(hidden_grad, first_full)
    input_grad = lax.psum_scatter(
        input_terms.astype(jnp.bfloat16), "mp", scatter_dimension=1, tiled=True
    )
    return (outputs, input_grad, first_grad, second_grad)


def solution(mesh):
    return jax.shard_map(
        shards,
        mesh=mesh,
        in_specs=(P("dp", "mp"), P("dp", "mp"), P("mp", "dp"), P("dp", "mp")),
        out_specs=(P("dp", "mp"), P("dp", "mp"), P("dp", "mp"), P("mp", "dp")),
        check_vma=False,
    )
```

profile of v0, /device:TPU:0, one launch (start us, length us, event | category | flops | bytes accessed | tf_op | source)
XLA Modules:
  0.0 851.3 jit_solution(15272797592748268866)
XLA Ops:
  7.2 0.0 all-gather.5.cloned.1.call-start
  7.2 0.7 all-gather.5.cloned.1.call-update
  7.9 0.0 all-gather.7.cloned.1.call-start
  7.9 0.7 all-gather.7.cloned.1.call-update
  8.6 0.0 all-gather.9.cloned.1.call-start
  8.7 0.7 all-gather.9.cloned.1.call-update
  9.4 0.0 all-gather.11.cloned.1.call-start
  9.4 0.5 all-gather.11.cloned.1.call-update
  10.0 0.0 reduce-scatter.13.cloned.1.call-start
  10.0 35.3 %all-gather.5.cloned.1.call-done = bf16[512,3072]{1,0:T(8,128)(2,1)} async-done(((bf16[512,384]{1,0:T(8,128)(2,1)}), bf16[512,3072]{1,0:T(8,128)(2,1)}) %all-gather.5.cloned.1.call-update) | async-done | bytes 3145744 | tf_op jit(solution)/shard_map/all_gather | solution.py:38
  45.3 168.3 %all-gather.7.cloned.1.call-done = bf16[3072,1536]{1,0:T(8,128)(2,1)} async-done(((bf16[768,1536]{1,0:T(8,128)(2,1)}), bf16[3072,1536]{1,0:T(8,128)(2,1)}) %all-gather.7.cloned.1.call-update) | async-done | bytes 9437200 | tf_op jit(solution)/shard_map/all_gather | solution.py:34
  213.7 10.5 %fusion.6 = f32[512,1536]{1,0:T(8,128)} fusion(bf16[512,3072]{1,0:T(8,128)(2,1)} %all-gather.5.cloned.1.call-done, bf16[3072,1536]{1,0:T(8,128)(2,1)} %all-gather.7.cloned.1.call-done), kind=kOutput, calls=%fused_computation.14 | convolution fusion | flops 4831838208 | bytes 15728640 | tf_op jit(solution)/shard_map/dot_general | solution.py:37
  224.2 156.0 %all-gather.9.cloned.1.call-done = bf16[1536,3072]{1,0:T(8,128)(2,1)} async-done(((bf16[1536,768]{1,0:T(8,128)(2,1)}), bf16[1536,3072]{1,0:T(8,128)(2,1)}) %all-gather.9.cloned.1.call-update) | async-done | bytes 9437200 | tf_op jit(solution)/shard_map/all_gather | solution.py:35
  380.2 9.4 %convolution_convert_fusion.3 = bf16[512,3072]{1,0:T(8,128)(2,1)S(1)} fusion(bf16[1536,3072]{1,0:T(8,128)(2,1)} %all-gather.9.cloned.1.call-done, f32[512,1536]{1,0:T(8,128)} %fusion.6), kind=kOutput, calls=%fused_computation.5 | convolution fusion | flops 4837343232 | bytes 15728640 | tf_op jit(solution)/shard_map/dot_general | solution.py:41
  389.6 2.8 copy.10
  392.4 0.0 copy-start.2
  392.4 0.0 reduce-scatter.13.cloned.1.call-update
  392.5 0.0 reduce-scatter.15.cloned.1.call-start
  392.5 20.4 %all-gather.11.cloned.1.call-done = bf16[512,3072]{1,0:T(8,128)(2,1)} async-done(((bf16[512,384]{1,0:T(8,128)(2,1)}), bf16[512,3072]{1,0:T(8,128)(2,1)}) %all-gather.11.cloned.1.call-update) | async-done | bytes 3145744 | tf_op jit(solution)/shard_map/all_gather | solution.py:45
  412.9 0.0 copy-done.2
  412.9 9.3 %fusion.5 = bf16[512,1536]{1,0:T(8,128)(2,1)S(1)} fusion(f32[512,1536]{1,0:T(8,128)S(1)} %copy-done.2, bf16[512,3072]{1,0:T(8,128)(2,1)} %all-gather.11.cloned.1.call-done, bf16[1536,3072]{1,0:T(8,128)(2,1)} %all-gather.9.cloned.1.call-done), kind=kOutput, calls=%fused_computation.13 | convolution fusion | flops 4839702528 | bytes 17301504 | tf_op jit(solution)/shard_map/dot_general | solution.py:28
  422.2 0.0 copy-start.3
  422.2 1.1 copy-done.3
  423.3 9.7 %convolution_convert_fusion.2 = bf16[512,3072]{1,0:T(8,128)(2,1)S(1)} fusion(bf16[512,1536]{1,0:T(8,128)(2,1)S(1)} %fusion.5, bf16[3072,1536]{1,0:T(8,128)(2,1)} %all-gather.7.cloned.1.call-done), kind=kOutput, calls=%fused_computation.4 | convolution fusion | flops 4833411072 | bytes 14155776 | tf_op jit(solution)/shard_map/dot_general | solution.py:28
  433.0 2.9 copy.12
  435.9 0.0 copy-start
  435.9 0.0 reduce-scatter.15.cloned.1.call-update
  435.9 0.0 reduce-scatter.9.cloned.1.call-start
  436.0 1.8 copy-done
  437.8 9.4 %fusion = bf16[3072,1536]{0,1:T(8,128)(2,1)} fusion(bf16[512,1536]{1,0:T(8,128)(2,1)} %copy-done.3, bf16[512,3072]{1,0:T(8,128)(2,1)S(1)} %copy-done), kind=kOutput, calls=%fused_computation.2 | convolution fusion | flops 4836556800 | bytes 14155776 | tf_op jit(solution)/shard_map/dot_general | solution.py:22
  447.2 0.0 copy-start.1
  447.2 0.0 reduce-scatter.9.cloned.1.call-update
  447.2 0.2 reduce-scatter.11.cloned.1.call-start
  447.4 1.7 copy-done.1
  449.1 9.5 %convolution_convert_fusion = bf16[1536,3072]{1,0:T(8,128)(2,1)} fusion(bf16[512,3072]{1,0:T(8,128)(2,1)S(1)} %copy-done.1, f32[512,1536]{1,0:T(8,128)} %fusion.6), kind=kOutput, calls=%fused_computation | convolution fusion | flops 4840488960 | bytes 15728640 | tf_op jit(solution)/shard_map/dot_general | solution.py:22
  458.7 0.0 reduce-scatter.11.cloned.1.call-update
  458.7 4.1 reduce-scatter.13.cloned.1.call-done
  462.8 1.9 copy.11
  464.7 47.4 %reduce-scatter.15.cloned.1.call-done = bf16[384,512]{1,0:T(8,128)(2,1)} async-done(((bf16[3072,512]{1,0:T(8,128)(2,1)}), bf16[384,512]{1,0:T(8,128)(2,1)}) %reduce-scatter.15.cloned.1.call-update) | async-done | bytes 393232
  512.1 1.9 copy.13
  514.0 161.7 %reduce-scatter.9.cloned.1.call-done = bf16[768,1536]{0,1:T(8,128)(2,1)} async-done(((bf16[3072,1536]{0,1:T(8,128)(2,1)}), bf16[768,1536]{0,1:T(8,128)(2,1)}) %reduce-scatter.9.cloned.1.call-update) | async-done | bytes 2359312 | tf_op jit(solution)/shard_map/reduce_scatter | solution.py:55
  675.7 4.6 copy.9
  680.3 160.0 %reduce-scatter.11.cloned.1.call-done = bf16[1536,768]{1,0:T(8,128)(2,1)} async-done(((bf16[1536,3072]{1,0:T(8,128)(2,1)}), bf16[1536,768]{1,0:T(8,128)(2,1)}) %reduce-scatter.11.cloned.1.call-update) | async-done | bytes 2359312 | tf_op jit(solution)/shard_map/reduce_scatter | solution.py:51
  840.2 4.2 convert_element_type.35
Async XLA Ops:
  7.2 38.2 %all-gather.5.cloned.1.call-start = ((), (), s32[]{:S(2)}) async-start(), calls=%async_computation.4 | async-start | bytes 3538944 | tf_op jit(solution)/shard_map/all_gather | solution.py:38
  7.9 205.8 %all-gather.7.cloned.1.call-start = ((), (), s32[]{:S(2)}) async-start(), calls=%async_computation.5 | async-start | bytes 11796480 | tf_op jit(solution)/shard_map/all_gather | solution.py:34
  8.6 371.6 %all-gather.9.cloned.1.call-start = ((), (), s32[]{:S(2)}) async-start(), calls=%async_computation.6 | async-start | bytes 11796480 | tf_op jit(solution)/shard_map/all_gather | solution.py:35
  9.4 403.5 %all-gather.11.cloned.1.call-start = ((), (), s32[]{:S(2)}) async-start(), calls=%async_computation.7 | async-start | bytes 3538944 | tf_op jit(solution)/shard_map/all_gather | solution.py:45
  10.0 452.8 %reduce-scatter.13.cloned.1.call-start = ((), (), s32[]{:S(2)}) async-start(), calls=%async_computation.10 | async-start | bytes 3538944
  392.4 20.5 %copy-start.2 = (f32[512,1536]{1,0:T(8,128)S(1)}, f32[512,1536]{1,0:T(8,128)}, u32[]{:S(2)}) copy-start(f32[512,1536]{1,0:T(8,128)} %fusion.6) | copy-start | bytes 9437188
  392.5 119.7 %reduce-scatter.15.cloned.1.call-start = ((), (), s32[]{:S(2)}) async-start(), calls=%async_computation.11 | async-start | bytes 3538944
  422.2 1.1 copy-start.3
  435.9 1.9 copy-start
  435.9 239.8 %reduce-scatter.9.cloned.1.call-start = ((), (), s32[]{:S(2)}) async-start(), calls=%async_computation.8 | async-start | bytes 11796480 | tf_op jit(solution)/shard_map/reduce_scatter | solution.py:55
  447.2 2.0 copy-start.1
  447.2 393.0 %reduce-scatter.11.cloned.1.call-start = ((), (), s32[]{:S(2)}) async-start(), calls=%async_computation.9 | async-start | bytes 11796480 | tf_op jit(solution)/shard_map/reduce_scatter | solution.py:51
Sparse Core Ops, SparseCore 0:
  9.8 35.4 all-gather.4
  46.9 166.7 all-gather.6
  215.2 164.9 all-gather.8
  381.9 30.8 all-gather.10
  416.7 46.0 reduce-scatter.12
  466.0 46.0 reduce-scatter.14
  514.5 161.1 reduce-scatter.8
  678.1 162.1 reduce-scatter.10
where the time goes:
time: 852 us; the launch traced here: 851 us
  waiting for transfers between devices  756 us (89%)
  matrix products  57.8 us (7%)
  local copies, waits for them, and re-layouts  18.7 us (2%)
  between operations  14.2 us (2%)
    all_gather x1, waiting for transfers between devices, shards(): first_full = lax.all_gather(w_first, 'dp', axis=0, tiled=True)  168 us
    reduce_scatter x1, waiting for transfers between devices, shards(): lax.psum_scatter(first_terms.astype(jnp.bfloat16), 'dp', scatter_dimensio...  162 us
    reduce_scatter x1, waiting for transfers between devices, shards(): lax.psum_scatter(second_terms.astype(jnp.bfloat16), 'dp', scatter_dimensi...  160 us
    all_gather x1, waiting for transfers between devices, shards(): second_full = lax.all_gather(w_second, 'dp', axis=1, tiled=True)  156 us
    unnamed x10, waiting for transfers between devices  54.2 us
    all_gather x1, waiting for transfers between devices, shards(): lax.all_gather(tokens, 'mp', axis=1, tiled=True)  35.3 us
    all_gather x1, waiting for transfers between devices, shards(): piece = lax.all_gather(cotangent, 'mp', axis=1, tiled=True)  20.4 us
    dot_general x2, matrix products, over_columns(): lax.dot_general(left, right, (((1,), (1,)), ((), ())), preferred_element_...  19 us
  transfers between devices with their start and end apart: 8, of which 8 were waited for; matrix products, arithmetic and copies ran while one was open for 8% of the time, Pallas kernels for 0%

commit v1 on v0

v1 whole, which is shorter than its diff:
```python
import jax
import jax.numpy as jnp
from jax import lax
from jax.experimental import pallas as pl
from jax.experimental.pallas import tpu as pltpu
from jax.sharding import PartitionSpec as P


inv_root_two = 0.7071067811865476
inv_root_tau = 0.3989422804014327


def gelu_value(value):
    return 0.5 * value * (1.0 + lax.erf(value * inv_root_two))


def gelu_slope(value):
    return (
        0.5 * (1.0 + lax.erf(value * inv_root_two))
        + value * jnp.exp(-0.5 * value * value) * inv_root_tau
    )


def product(left, right, left_dim, right_dim):
    return lax.dot_general(
        left, right, (((left_dim,), (right_dim,)), ((), ())), preferred_element_type=jnp.float32
    )


def rearrange(inputs, moves, out_shapes, scalars):
    def aligned(place, tile):
        return (place[1] if isinstance(place, tuple) else place) % tile == 0

    if all(
        aligned(value, tile)
        for move in moves
        for value, tile in zip(move[1:3] + move[4:8], (16, 128) * 3)
    ):
        tables = jnp.stack([jnp.asarray(s, jnp.int32) for s in scalars])

        def kernel(table, *refs):
            sources, targets, sems = refs[: len(inputs)], refs[len(inputs) : -1], refs[-1]

            def place(value, tile):
                if isinstance(value, tuple):
                    return pl.multiple_of(table[value[0]] * value[1], tile)
                return value

            copies = []
            for i, (a, ar, ac, b, br, bc, rows, columns) in enumerate(moves):
                copies.append(
                    pltpu.make_async_copy(
                        sources[a].at[pl.ds(place(ar, 16), rows), pl.ds(place(ac, 128), columns)],
                        targets[b].at[pl.ds(place(br, 16), rows), pl.ds(place(bc, 128), columns)],
                        sems.at[i],
                    )
                )
                copies[-1].start()
            for copy in copies:
                copy.wait()

        size = sum(r * c for r, c in out_shapes)
        return pl.pallas_call(
            kernel,
            out_shape=[jax.ShapeDtypeStruct(s, jnp.bfloat16) for s in out_shapes],
            in_specs=[pl.BlockSpec(memory_space=pltpu.SMEM)]
            + [pl.BlockSpec(memory_space=pl.ANY)] * len(inputs),
            out_specs=[pl.BlockSpec(memory_space=pltpu.VMEM)] * len(out_shapes),
            scratch_shapes=[pltpu.SemaphoreType.DMA((len(moves),))],
            cost_estimate=pl.CostEstimate(flops=0, transcendentals=0, bytes_accessed=4 * size),
        )(tables, *inputs)

    def at(value):
        return scalars[value[0]] * value[1] if isinstance(value, tuple) else value

    outputs = [jnp.zeros(s, jnp.bfloat16) for s in out_shapes]
    for a, ar, ac, b, br, bc, rows, columns in moves:
        block = lax.dynamic_slice(inputs[a], (at(ar), at(ac)), (rows, columns))
        outputs[b] = lax.dynamic_update_slice(outputs[b], block, (at(br), at(bc)))
    return outputs


def add(*terms):
    return sum(t.astype(jnp.float32) for t in terms).astype(jnp.bfloat16)


def body(n_dp, n_mp):
    n_chips = n_mp // 2
    if n_chips != n_dp or n_dp & (n_dp - 1) or n_dp < 4:
        raise ValueError("mesh shape")
    places = range(n_dp)

    def move(value, dz, dm):
        pairs = [
            (z * n_mp + m, (z ^ dz) * n_mp + (m ^ dm)) for z in range(n_dp) for m in range(n_mp)
        ]
        return lax.ppermute(value, ("dp", "mp"), pairs)

    z_masks = []
    span = n_dp
    while span > 1:
        z_masks.append(span - 1)
        span //= 2
    near = [0]
    for mask in z_masks[:-1]:
        near += [j ^ mask for j in near]
    groups = [[j ^ z_masks[-1] for j in near], near]
    bits = [1 << i for i in range(n_chips.bit_length() - 1)]

    def gather_z(own):
        blocks = {0: own}
        for mask in z_masks:
            blocks.update({j ^ mask: move(b, mask, 0) for j, b in list(blocks.items())})
        return blocks

    def reduce_z(blocks):
        blocks = dict(blocks)
        for i in reversed(range(len(z_masks))):
            kept = [0]
            for earlier in z_masks[:i]:
                kept += [j ^ earlier for j in kept]
            arrived = {}
            for j in kept:
                far = j ^ z_masks[i]
                arrived[j] = move(blocks.pop(far), z_masks[i], 0)
            for j in kept:
                blocks[j] = add(blocks[j], arrived[j])
        return blocks[0]

    def gather_chips(own):
        half, width = own.shape[0] // 2, own.shape[1]
        a = move(own, 0, 2 * bits[0])
        b = move(own, 0, 2 * bits[1])
        upper, lower = rearrange(
            [a, b],
            [(0, 0, 0, 0, 0, 0, half, width), (1, half, 0, 1, 0, 0, half, width)],
            [(half, width)] * 2,
            [0],
        )
        upper = move(upper, 0, 2 * bits[1])
        lower = move(lower, 0, 2 * bits[0])
        known = [(0, 0, own), (1, 0, a), (2, 0, b), (3, 0, upper), (3, half, lower)]
        for bit in bits[2:]:
            known += [(r ^ bit, row, move(x, 0, 2 * bit)) for r, row, x in known]
        return known

    def reduce_chips(blocks, parts):
        blocks = dict(blocks)
        for bit in reversed(bits[2:]):
            for r, row in [k for k in blocks if k[0] & bit]:
                arrived = move(blocks.pop((r, row)), 0, 2 * bit)
                blocks[r ^ bit, row] = add(blocks[r ^ bit, row], arrived)
        half = blocks[0, 0].shape[0] // 2
        upper = move(blocks[3, 0], 0, 2 * bits[0])
        lower = move(blocks[3, 1], 0, 2 * bits[1])
        to_b = jnp.concatenate([add(blocks[2, 0][:half], upper), blocks[2, 0][half:]])
        from_b = move(to_b, 0, 2 * bits[1])
        to_a = jnp.concatenate([blocks[1, 0][:half], add(blocks[1, 0][half:], lower)])
        from_a = move(to_a, 0, 2 * bits[0])
        rows = 2 * half // parts
        return [
            add(*(x[i * rows : (i + 1) * rows] for x in (blocks[0, 0], from_a, from_b)))
            for i in range(parts)
        ]

    def shards(tokens, w_first, w_second, cotangent):
        z, m = lax.axis_index("dp"), lax.axis_index("mp")
        core = m & 1
        shift = z ^ (m >> 1)
        rows, width = tokens.shape
        units = w_first.shape[1] // n_dp
        features = n_chips * width
        by_z = [z ^ j for j in places]
        by_shift = [shift ^ j for j in places]
        scalars = [core, 1 - core] + by_z + by_shift
        z_at, shift_at = 2, 2 + n_dp

        def spread(array, unit_dim):
            def turned(pair):
                return pair if unit_dim == 1 else pair[::-1]

            def moved(a, source, b, target, size):
                return (a, *turned(source), b, *turned(target), *turned(size))

            other = lax.dynamic_slice(
                array, turned(((1 - core) * width, 0)), turned((width, n_dp * units))
            )
            other = move(other, 0, 1)
            parts = rearrange(
                [array, other],
                [
                    moved(c, (((0, width), 0)[c], (z_at + j, units)), j, (0, c * units), (width, units))
                    for j in places
                    for c in range(2)
                ],
                [turned((width, 2 * units))] * n_dp,
                scalars,
            )
            parts = [parts[0]] + [move(parts[j], j, 0) for j in places if j]
            return rearrange(
                parts,
                [
                    moved(j, (0, 0), 0, ((shift_at + j, width), 0), (width, 2 * units))
                    for j in places
                ],
                [turned((features, 2 * units))],
                scalars,
            )[0]

        def unspread(array, unit_dim):
            def turned(pair):
                return pair if unit_dim == 1 else pair[::-1]

            def moved(a, source, b, target, size):
                return (a, *turned(source), b, *turned(target), *turned(size))

            other = move(lax.slice(array, turned((0, units)), turned((features, 2 * units))), 0, 1)
            parts = rearrange(
                [array, other],
                [
                    moved(c, ((shift_at + j, width), 0), j, ((c, width), 0), (width, units))
                    for j in places
                    for c in range(2)
                ],
                [turned((2 * width, units))] * n_dp,
                scalars,
            )
            result = jnp.zeros(turned((2 * width, n_dp * units)), jnp.float32)
            for j in (0, *reversed(places[1:])):
                part = move(parts[j], j, 0) if j else parts[j]
                result = lax.dynamic_update_slice(
                    result, part.astype(jnp.float32), turned((0, by_z[j] * units))
                )
            return result

        def gather(own):
            known = gather_z(own)
            blocks, moves = [], []
            for g in (1, 0):
                size = len(groups[g])
                joined = rearrange(
                    [known[j] for j in groups[g]],
                    [(i, 0, 0, 0, i * rows, 0, rows, width) for i in range(size)],
                    [(size * rows, width)],
                    [0],
                )[0]
                for r, row, block in gather_chips(joined):
                    moves.append(
                        (len(blocks), 0, 0, 0, g * size * rows + row, r * width, block.shape[0], width)
                    )
                    blocks.append(block)
            return rearrange(blocks, moves, [(n_dp * rows, features)], [0])[0]

        def reduce(share):
            size = n_dp * rows // 2
            keys, moves, shapes = [], [], []
            for g in range(2):
                for r in range(n_chips):
                    for row in range(2) if r & 3 == 3 else range(1):
                        count = size // 2 if r & 3 == 3 else size
                        moves.append(
                            (0, g * size + row * count, r * width, len(keys), 0, 0, count, width)
                        )
                        keys.append((g, r, row))
                        shapes.append((count, width))
            blocks = dict(zip(keys, rearrange([share], moves, shapes, [0])))
            known = {}
            for g in range(2):
                mine = {k[1:]: v for k, v in blocks.items() if k[0] == g}
                known.update(zip(groups[g], reduce_chips(mine, len(groups[g]))))
            return reduce_z(known)

        def over_cores(share):
            return share[:, :units] + move(share[:, units:], 0, 1)

        def both(half):
            return jnp.concatenate([half, move(half, 0, 1)], axis=1)

        inputs_all = gather(tokens)
        first = spread(w_first, 1)
        piece = gather(cotangent)
        second = spread(w_second, 0)
        share = product(inputs_all, first, 1, 0)
        pre_act = over_cores(share)
        half = gelu_value(pre_act).astype(jnp.bfloat16)
        half, slope = lax.optimization_barrier((half, gelu_slope(pre_act)))
        activated = both(half)
        second_terms = product(activated, piece, 0, 0).astype(jnp.bfloat16)
        second_grad = unspread(second_terms, 0)
        share = product(activated, second, 1, 0).astype(jnp.bfloat16)
        outputs = reduce(share)
        share = product(piece, second, 1, 1)
        back_pre = over_cores(share)
        half = (back_pre * slope).astype(jnp.bfloat16)
        hidden_grad = both(half)
        first_terms = product(inputs_all, hidden_grad, 0, 0).astype(jnp.bfloat16)
        first_grad = unspread(first_terms, 1)
        share = product(hidden_grad, first, 1, 1).astype(jnp.bfloat16)
        input_grad = reduce(share)
        return (outputs, input_grad, first_grad, second_grad)

    return shards


def solution(mesh):
    return jax.shard_map(
        body(mesh.shape["dp"], mesh.shape["mp"]),
        mesh=mesh,
        in_specs=(P("dp", "mp"), P("dp", "mp"), P("mp", "dp"), P("dp", "mp")),
        out_specs=(P("dp", "mp"), P("dp", "mp"), P("dp", "mp"), P("mp", "dp")),
        check_vma=False,
    )
```

time: 852 us -> 514 us (0.60)
  waiting for transfers between devices: 756 us -> 207 us
  starting transfers between devices: 0.5 us -> 137 us
  Pallas kernels: 0 us -> 61.2 us
  other arithmetic: 4.21 us -> 28.2 us
  between operations: 14.2 us -> 1.62 us
  local copies, waits for them, and re-layouts: 18.7 us -> 27.8 us
  matrix products: 57.8 us -> 49.1 us
    all_gather x4 -> x0, waiting for transfers between devices: 380 us -> none  [the longest x1 168 us: shards(): first_full = lax.all_gather(w_first, 'dp', axis=0, tiled=True)]
    reduce_scatter x2 -> x0, waiting for transfers between devices: 322 us -> none  [the longest x1 162 us: shards(): lax.psum_scatter(first_terms.astype(jnp.bfloat16), 'dp', scatter_dimensio...]
    ppermute x0 -> x64, waiting for transfers between devices: none -> 207 us  [move(): return lax.ppermute(value, ('dp', 'mp'), pairs)]
    ppermute x0 -> x64, starting transfers between devices: none -> 137 us  [move(): return lax.ppermute(value, ('dp', 'mp'), pairs)]
    pallas_call x0 -> x18, Pallas kernels: none -> 61.2 us  [rearrange(): pl.pallas_call(kernel, out_shape=[jax.ShapeDtypeStruct(s, jnp.bfloat16) f...]
    unnamed x10 -> x0, waiting for transfers between devices: 54.2 us -> none
    convert_element_type x1 -> x15, other arithmetic: 4.21 us -> 15 us  [the longest x14 10.6 us: add(): return sum((t.astype(jnp.float32) for t in terms)).astype(jnp.bfloat16)]
    slice x0 -> x12, local copies, waits for them, and re-layouts: none -> 10.8 us  [the longest x4 4.17 us: reduce_chips(): blocks[2, 0][half:]]
  transfers between devices with their start and end apart: 8 -> 64, of which waited for: 8 -> 26; matrix products, arithmetic and copies ran while one was open for 8% -> 19% of each run, Pallas kernels for 0% -> 12%
where the time goes in v1:
time: 514 us; the launch traced here: 512 us
  waiting for transfers between devices  207 us (40%)
  starting transfers between devices  137 us (27%)
  Pallas kernels  61.2 us (12%)
  matrix products  49.1 us (10%)
  other arithmetic  28.2 us (5%)
  local copies, waits for them, and re-layouts  27.8 us (5%)
    ppermute x64, waiting for transfers between devices, move(): return lax.ppermute(value, ('dp', 'mp'), pairs)  207 us
    ppermute x64, starting transfers between devices, move(): return lax.ppermute(value, ('dp', 'mp'), pairs)  137 us
    pallas_call x18, Pallas kernels, rearrange(): pl.pallas_call(kernel, out_shape=[jax.ShapeDtypeStruct(s, jnp.bfloat16) f...  61.2 us
    dot_general x6, matrix products, product(): lax.dot_general(left, right, (((left_dim,), (right_dim,)), ((), ())), pre...  49.1 us
    convert_element_type x14, other arithmetic, add(): return sum((t.astype(jnp.float32) for t in terms)).astype(jnp.bfloat16)  10.6 us
  transfers between devices with their start and end apart: 64, of which 26 were waited for; matrix products, arithmetic and copies ran while one was open for 19% of the time, Pallas kernels for 12%

profile of v1, /device:TPU:0, one launch (start us, length us, event | category | flops | bytes accessed | tf_op | source)
XLA Modules:
  0.0 511.7 jit_solution(5379527648948461375)
XLA Ops:
  0.6 5.1 %collective-permute-start = (bf16[512,384]{1,0:T(8,128)(2,1)}, bf16[512,384]{1,0:T(8,128)(2,1)}, u32[]{:S(2)}, u32[]{:S(2)}) collective-permute-start(bf16[512,384]{1,0:T(8,128)(2,1)} %refs_0_.4), channel_id=1, source_target_pairs={{0,24},{1,25},{2,26},{3,27},{4,28},{5,29},{6,30},{7,31},{8,16},{9,... | collective-permute-start | bytes 1179656 | tf_op jit(solution)/shard_map/ppermute | solution.py:97
  10.2 6.0 %collective-permute-done.refs_1_ = bf16[512,384]{1,0:T(8,128)(2,1)} collective-permute-done((bf16[512,384]{1,0:T(8,128)(2,1)}, bf16[512,384]{1,0:T(8,128)(2,1)}, u32[]{:S(2)}, u32[]{:S(2)}) %collective-permute-start) | collective-permute-done | bytes 393248 | tf_op jit(solution)/shard_map/ppermute | solution.py:97
  16.2 9.0 %collective-permute-start.6 = (bf16[512,384]{1,0:T(8,128)(2,1)}, bf16[512,384]{1,0:T(8,128)(2,1)}, u32[]{:S(2)}, u32[]{:S(2)}) collective-permute-start(bf16[512,384]{1,0:T(8,128)(2,1)} %collective-permute-done.refs_1_), channel_id=1, source_target_pairs={{0,8},{1,9},{2,10},{3,11},{4,12},{5,13},{6,14},{7,15},{8,0},{9,1},... | collective-permute-start | bytes 1179656 | tf_op jit(solution)/shard_map/ppermute | solution.py:97
  27.2 4.2 collective-permute-done.5.refs_0_
  33.9 7.0 %collective-permute-done.37.refs_0_ = bf16[512,384]{1,0:T(8,128)(2,1)S(1)} collective-permute-done((bf16[512,384]{1,0:T(8,128)(2,1)}, bf16[512,384]{1,0:T(8,128)(2,1)S(1)}, u32[]{:S(2)}, u32[]{:S(2)}) %collective-permute-start.37) | collective-permute-done | bytes 393248 | tf_op jit(solution)/shard_map/ppermute | solution.py:97
  42.5 6.6 %collective-permute-done.6.refs_1_ = bf16[512,384]{1,0:T(8,128)(2,1)} collective-permute-done((bf16[512,384]{1,0:T(8,128)(2,1)}, bf16[512,384]{1,0:T(8,128)(2,1)}, u32[]{:S(2)}, u32[]{:S(2)}) %collective-permute-start.6) | collective-permute-done | bytes 393248 | tf_op jit(solution)/shard_map/ppermute | solution.py:97
  52.8 7.6 %collective-permute-done.38.refs_1_ = bf16[512,384]{1,0:T(8,128)(2,1)} collective-permute-done((bf16[512,384]{1,0:T(8,128)(2,1)}, bf16[512,384]{1,0:T(8,128)(2,1)}, u32[]{:S(2)}, u32[]{:S(2)}) %collective-permute-start.38) | collective-permute-done | bytes 393248 | tf_op jit(solution)/shard_map/ppermute | solution.py:97
  72.2 8.8 %collective-permute-done.33.refs_0_.refs_1_ = bf16[1024,384]{1,0:T(8,128)(2,1)S(1)} collective-permute-done((bf16[1024,384]{1,0:T(8,128)(2,1)}, bf16[1024,384]{1,0:T(8,128)(2,1)S(1)}, u32[]{:S(2)}, u32[]{:S(2)}) %collective-permute-start.33) | collective-permute-done | bytes 786464 | tf_op jit(solution)/shard_map/ppermute | solution.py:97
  84.7 3.8 shard_map.80
  88.5 19.3 %collective-permute-done.3.refs_3_ = bf16[512,384]{1,0:T(8,128)(2,1)S(1)} collective-permute-done((bf16[512,384]{1,0:T(8,128)(2,1)}, bf16[512,384]{1,0:T(8,128)(2,1)S(1)}, u32[]{:S(2)}, u32[]{:S(2)}) %collective-permute-start.3) | collective-permute-done | bytes 393248 | tf_op jit(solution)/shard_map/ppermute | solution.py:97
  108.9 3.3 collective-permute-start.14
  112.2 3.7 shard_map.82
  116.0 6.5 %collective-permute-done.40.refs_1_.refs_7_ = bf16[1024,384]{1,0:T(8,128)(2,1)S(1)} collective-permute-done((bf16[1024,384]{1,0:T(8,128)(2,1)}, bf16[1024,384]{1,0:T(8,128)(2,1)S(1)}, u32[]{:S(2)}, u32[]{:S(2)}) %collective-permute-start.40) | collective-permute-done | bytes 786464 | tf_op jit(solution)/shard_map/ppermute | solution.py:97
  124.9 13.9 %collective-permute-done.12.refs_1_ = bf16[384,768]{1,0:T(8,128)(2,1)} collective-permute-done((bf16[384,768]{1,0:T(8,128)(2,1)}, bf16[384,768]{1,0:T(8,128)(2,1)}, u32[]{:S(2)}, u32[]{:S(2)}) %collective-permute-start.12) | collective-permute-done | bytes 589856 | tf_op jit(solution)/shard_map/ppermute | solution.py:97
  138.7 12.5 %collective-permute-done.13.refs_2_ = bf16[384,768]{1,0:T(8,128)(2,1)} collective-permute-done((bf16[384,768]{1,0:T(8,128)(2,1)}, bf16[384,768]{1,0:T(8,128)(2,1)}, u32[]{:S(2)}, u32[]{:S(2)}) %collective-permute-start.13) | collective-permute-done | bytes 589856 | tf_op jit(solution)/shard_map/ppermute | solution.py:97
  157.4 3.7 shard_map.81
  165.2 5.4 %shard_map.79 = bf16[2048,1536]{1,0:T(8,128)(2,1)} custom-call(s32[1]{0:T(128)} %constant.16.clone.1.table, bf16[1024,384]{1,0:T(8,128)(2,1)} %shard_map.75.refs_0_, bf16[1024,384]{1,0:T(8,128)(2,1)} %copy-done.9, bf16[1024,384]{1,0:T(8,128)(2,1)} %copy-done.10, bf16[512,384]{1,0:T(8,128)(2,1)} %copy-done.39, bf16[512,384]{1,0:T(8,128)(2,1)} %copy-done.41, ...), custom_call_target="tpu_custom_call" | custom-call | bytes 12582912 | tf_op jit(solution)/shard_map/pallas_call | solution.py:63
  171.6 28.4 %collective-permute-done.19.refs_2_ = bf16[768,384]{1,0:T(8,128)(2,1)} collective-permute-done((bf16[768,384]{1,0:T(8,128)(2,1)}, bf16[768,384]{1,0:T(8,128)(2,1)}, u32[]{:S(2)}, u32[]{:S(2)}) %collective-permute-start.19) | collective-permute-done | bytes 589856 | tf_op jit(solution)/shard_map/ppermute | solution.py:97
  200.9 7.1 %fusion.8 = f32[2048,768]{1,0:T(8,128)S(1)} fusion(bf16[2048,1536]{1,0:T(8,128)(2,1)} %shard_map.79, bf16[1536,768]{1,0:T(8,128)(2,1)S(1)} %copy-done.13), kind=kOutput, calls=%fused_computation.60 | convolution fusion | flops 4831838208 | bytes 14942208 | tf_op jit(solution)/shard_map/dot_general | solution.py:25
  210.6 3.7 shard_map.83
  215.0 5.5 %shard_map.89 = bf16[2048,1536]{1,0:T(8,128)(2,1)} custom-call(s32[1]{0:T(128)} %constant.16.clone.1.table, bf16[1024,384]{1,0:T(8,128)(2,1)} %shard_map.85.refs_0_, bf16[1024,384]{1,0:T(8,128)(2,1)} %copy-done.7, bf16[1024,384]{1,0:T(8,128)(2,1)} %copy-done.8, bf16[512,384]{1,0:T(8,128)(2,1)} %copy-done.40, ...), custom_call_target="tpu_custom_call" | custom-call | bytes 12582912 | tf_op jit(solution)/shard_map/pallas_call | solution.py:63
  220.6 7.9 %fusion.9 = f32[2048,768]{1,0:T(8,128)S(1)} fusion(bf16[2048,1536]{1,0:T(8,128)(2,1)} %shard_map.89, bf16[768,1536]{1,0:T(8,128)(2,1)} %shard_map.83), kind=kOutput, calls=%fused_computation.61 | convolution fusion | flops 4831838208 | bytes 14942208 | tf_op jit(solution)/shard_map/dot_general | solution.py:25
  232.7 4.5 fusion.3
  238.3 4.4 fusion.5
  248.3 6.8 %convolution_convert_fusion.1.refs_0_ = bf16[2048,1536]{1,0:T(8,128)(2,1)} fusion(bf16[2048,768]{1,0:T(8,128)(2,1)S(1)} %constant_dynamic-update-slice_fusion, bf16[768,1536]{1,0:T(8,128)(2,1)S(1)} %copy-done.15), kind=kOutput, calls=%fused_computation.1 | convolution fusion | flops 4834983936 | bytes 11796480 | tf_op jit(solution)/shard_map/dot_general | solution.py:25
  255.1 5.6 %shard_map.84 = (bf16[1024,384]{1,0:T(8,128)(2,1)}, bf16[1024,384]{1,0:T(8,128)(2,1)}, bf16[1024,384]{1,0:T(8,128)(2,1)}, bf16[512,384]{1,0:T(8,128)(2,1)}, bf16...) custom-call(s32[1]{0:T(128)} %constant.16.clone.1.table, ...), custom_call_target="tpu_custom_call" | custom-call | bytes 12582912 | tf_op jit(solution)/shard_map/pallas_call | solution.py:63
  267.0 8.6 %convolution_convert_fusion.2.refs_0_ = bf16[768,1536]{1,0:T(8,128)(2,1)S(1)} fusion(bf16[2048,768]{1,0:T(8,128)(2,1)} %copy-done.19, bf16[2048,1536]{1,0:T(8,128)(2,1)} %shard_map.89), kind=kOutput, calls=%fused_computation.3 | convolution fusion | flops 4833017856 | bytes 11796480 | tf_op jit(solution)/shard_map/dot_general | solution.py:25
  275.7 9.6 %convolution_convert_fusion.3.refs_0_ = bf16[1536,768]{1,0:T(8,128)(2,1)} fusion(bf16[2048,1536]{1,0:T(8,128)(2,1)S(1)} %bitcast.21, bf16[2048,384]{1,0:T(8,128)(2,1)} %collective-permute-done.44, bf16[2048,384]{1,0:T(8,128)(2,1)} %fusion.5), kind=kOutput, calls=%fused_computation.4 | convolution fusion | flops 4839309312 | bytes 11796480 | tf_op jit(solution)/shard_map/dot_general | solution.py:25
  285.3 9.1 %convolution_convert_fusion.refs_0_ = bf16[2048,1536]{1,0:T(8,128)(2,1)} fusion(bf16[1536,768]{1,0:T(8,128)(2,1)S(1)} %copy-done.14, bf16[2048,384]{1,0:T(8,128)(2,1)} %collective-permute-done.44, bf16[2048,384]{1,0:T(8,128)(2,1)} %fusion.5), kind=kOutput, calls=%fused_computation | convolution fusion | flops 4841275392 | bytes 11796480 | tf_op jit(solution)/shard_map/dot_general | solution.py:25
  295.2 5.6 %shard_map.90 = (bf16[1024,384]{1,0:T(8,128)(2,1)}, bf16[1024,384]{1,0:T(8,128)(2,1)}, bf16[1024,384]{1,0:T(8,128)(2,1)}, bf16[512,384]{1,0:T(8,128)(2,1)}, bf16...) custom-call(s32[1]{0:T(128)} %constant.16.clone.1.table, ...), custom_call_target="tpu_custom_call" | custom-call | bytes 12582912 | tf_op jit(solution)/shard_map/pallas_call | solution.py:63
  317.0 2.6 collective-permute-done.49
  332.5 3.9 shard_map.91
  337.4 3.7 shard_map.92
  341.2 3.7 collective-permute-done.28
  350.2 11.6 %collective-permute-done.52 = bf16[1024,384]{1,0:T(8,128)(2,1)} collective-permute-done((bf16[1024,384]{1,0:T(8,128)(2,1)}, bf16[1024,384]{1,0:T(8,128)(2,1)}, u32[]{:S(2)}, u32[]{:S(2)}) %collective-permute-start.52) | collective-permute-done | bytes 786464 | tf_op jit(solution)/shard_map/ppermute | solution.py:97
  363.7 8.1 %collective-permute-start.30 = (bf16[512,384]{1,0:T(8,128)(2,1)S(1)}, bf16[512,384]{1,0:T(8,128)(2,1)S(1)}, u32[]{:S(2)}, u32[]{:S(2)}) collective-permute-start(bf16[512,384]{1,0:T(8,128)(2,1)S(1)} %get-tuple-element.101), channel_id=1, source_target_pairs={{0,8},{1,9},{2,10},{3,11},{4,12},{5,13},{6,14},{7,15},{8,0},{9,1},... | collective-permute-start | bytes 1179656 | tf_op jit(solution)/shard_map/ppermute | solution.py:97
  373.5 5.0 collective-permute-done.24
  378.5 2.6 collective-permute-start.57
  381.1 7.5 %collective-permute-start.54 = (bf16[512,384]{1,0:T(8,128)(2,1)S(1)}, bf16[512,384]{1,0:T(8,128)(2,1)S(1)}, u32[]{:S(2)}, u32[]{:S(2)}) collective-permute-start(bf16[512,384]{1,0:T(8,128)(2,1)S(1)} %get-tuple-element.99), channel_id=1, source_target_pairs={{0,8},{1,9},{2,10},{3,11},{4,12},{5,13},{6,14},{7,15},{8,0},{9,1},... | collective-permute-start | bytes 1179656 | tf_op jit(solution)/shard_map/ppermute | solution.py:97
  393.2 7.8 %collective-permute-start.58 = (bf16[768,384]{1,0:T(8,128)(2,1)S(1)}, bf16[768,384]{1,0:T(8,128)(2,1)S(1)}, u32[]{:S(2)}, u32[]{:S(2)}) collective-permute-start(bf16[768,384]{1,0:T(8,128)(2,1)S(1)} %copy-done.47), channel_id=1, source_target_pairs={{0,16},{1,17},{2,18},{3,19},{4,20},{5,21},{6,22},{7,23},{8,24},{9,... | collective-permute-start | bytes 1769480 | tf_op jit(solution)/shard_map/ppermute | solution.py:97
  401.3 9.9 %collective-permute-done.54 = bf16[512,384]{1,0:T(8,128)(2,1)S(1)} collective-permute-done((bf16[512,384]{1,0:T(8,128)(2,1)S(1)}, bf16[512,384]{1,0:T(8,128)(2,1)S(1)}, u32[]{:S(2)}, u32[]{:S(2)}) %collective-permute-start.54) | collective-permute-done | bytes 393248 | tf_op jit(solution)/shard_map/ppermute | solution.py:97
  411.4 20.2 %collective-permute-start.63 = (bf16[384,768]{1,0:T(8,128)(2,1)S(1)}, bf16[384,768]{1,0:T(8,128)(2,1)S(1)}, u32[]{:S(2)}, u32[]{:S(2)}) collective-permute-start(bf16[384,768]{1,0:T(8,128)(2,1)S(1)} %copy-done.46), channel_id=1, source_target_pairs={{0,8},{1,9},{2,10},{3,11},{4,12},{5,13},{6,14},{7,15},{8,0},{9,1},... | collective-permute-start | bytes 1769480 | tf_op jit(solution)/shard_map/ppermute | solution.py:97
  431.8 25.1 %collective-permute-start.29 = (bf16[512,384]{1,0:T(8,128)(2,1)S(1)}, bf16[512,384]{1,0:T(8,128)(2,1)S(1)}, u32[]{:S(2)}, u32[]{:S(2)}) collective-permute-start(bf16[512,384]{1,0:T(8,128)(2,1)S(1)} %get-tuple-element.100), channel_id=1, source_target_pairs={{0,8},{1,9},{2,10},{3,11},{4,12},{5,13},{6,14},{7,15},{8,0},{9,1},... | collective-permute-start | bytes 1179656 | tf_op jit(solution)/shard_map/ppermute | solution.py:97
  457.0 12.1 %collective-permute-done.58 = bf16[768,384]{1,0:T(8,128)(2,1)S(1)} collective-permute-done((bf16[768,384]{1,0:T(8,128)(2,1)S(1)}, bf16[768,384]{1,0:T(8,128)(2,1)S(1)}, u32[]{:S(2)}, u32[]{:S(2)}) %collective-permute-start.58) | collective-permute-done | bytes 589856 | tf_op jit(solution)/shard_map/ppermute | solution.py:97
  469.3 10.8 %collective-permute-done.62 = bf16[384,768]{1,0:T(8,128)(2,1)S(1)} collective-permute-done((bf16[384,768]{1,0:T(8,128)(2,1)S(1)}, bf16[384,768]{1,0:T(8,128)(2,1)S(1)}, u32[]{:S(2)}, u32[]{:S(2)}) %collective-permute-start.62) | collective-permute-done | bytes 589856 | tf_op jit(solution)/shard_map/ppermute | solution.py:97
  480.1 3.0 collective-permute-start.31
  484.4 21.0 %collective-permute-done.29 = bf16[512,384]{1,0:T(8,128)(2,1)S(1)} collective-permute-done((bf16[512,384]{1,0:T(8,128)(2,1)S(1)}, bf16[512,384]{1,0:T(8,128)(2,1)S(1)}, u32[]{:S(2)}, u32[]{:S(2)}) %collective-permute-start.29) | collective-permute-done | bytes 393248 | tf_op jit(solution)/shard_map/ppermute | solution.py:97
  506.4 4.3 collective-permute-done.53
  (268 shorter events, 113.7 us)
Async XLA Ops:
  5.8 25.7 %collective-permute-start.5 = (bf16[512,384]{1,0:T(8,128)(2,1)}, bf16[512,384]{1,0:T(8,128)(2,1)}, u32[]{:S(2)}, u32[]{:S(2)}) collective-permute-start(bf16[512,384]{1,0:T(8,128)(2,1)} %refs_0_.4), channel_id=1, source_target_pairs={{0,8},{1,9},{2,10},{3,11},{4,12},{5,13},{6,14},{7,15},{8,0},{9,1},... | collective-permute-start | bytes 1179656 | tf_op jit(solution)/shard_map/ppermute | solution.py:97
  5.8 28.1 %collective-permute-start.32 = (bf16[512,384]{1,0:T(8,128)(2,1)}, bf16[512,384]{1,0:T(8,128)(2,1)}, u32[]{:S(2)}, u32[]{:S(2)}) collective-permute-start(bf16[512,384]{1,0:T(8,128)(2,1)} %refs_0_.7), channel_id=1, source_target_pairs={{0,24},{1,25},{2,26},{3,27},{4,28},{5,29},{6,30},{7,31},{8,16},{9,... | collective-permute-start | bytes 1179656 | tf_op jit(solution)/shard_map/ppermute | solution.py:97
  6.7 34.2 %collective-permute-start.37 = (bf16[512,384]{1,0:T(8,128)(2,1)}, bf16[512,384]{1,0:T(8,128)(2,1)S(1)}, u32[]{:S(2)}, u32[]{:S(2)}) collective-permute-start(bf16[512,384]{1,0:T(8,128)(2,1)} %refs_0_.7), channel_id=1, source_target_pairs={{0,8},{1,9},{2,10},{3,11},{4,12},{5,13},{6,14},{7,15},{8,0},{9,1},... | collective-permute-start | bytes 1179656 | tf_op jit(solution)/shard_map/ppermute | solution.py:97
  10.2 55.9 %collective-permute-start.11 = (bf16[384,1536]{1,0:T(8,128)(2,1)}, bf16[384,1536]{1,0:T(8,128)(2,1)}, u32[]{:S(2)}, u32[]{:S(2)}) collective-permute-start(bf16[384,1536]{1,0:T(8,128)(2,1)} %constant_dynamic-slice_fusion.1), channel_id=1, source_target_pairs={{0,1},{1,0},{2,3},{3,2},{4,5},{5,4},{6,7},{7,6},{8,9},{9,8},{10,11... | collective-permute-start | bytes 3538952 | tf_op jit(solution)/shard_map/ppermute | solution.py:97
  16.2 32.9 %collective-permute-start.6 = (bf16[512,384]{1,0:T(8,128)(2,1)}, bf16[512,384]{1,0:T(8,128)(2,1)}, u32[]{:S(2)}, u32[]{:S(2)}) collective-permute-start(bf16[512,384]{1,0:T(8,128)(2,1)} %collective-permute-done.refs_1_), channel_id=1, source_target_pairs={{0,8},{1,9},{2,10},{3,11},{4,12},{5,13},{6,14},{7,15},{8,0},{9,1},... | collective-permute-start | bytes 1179656 | tf_op jit(solution)/shard_map/ppermute | solution.py:97
  31.5 30.4 %collective-permute-start.1 = (bf16[1024,384]{1,0:T(8,128)(2,1)}, bf16[1024,384]{1,0:T(8,128)(2,1)S(1)}, u32[]{:S(2)}, u32[]{:S(2)}) collective-permute-start(bf16[1024,384]{1,0:T(8,128)(2,1)} %shard_map.75.refs_0_), channel_id=1, source_target_pairs={{0,2},{1,3},{2,0},{3,1},{4,6},{5,7},{6,4},{7,5},{8,10},{9,11},{10,... | collective-permute-start | bytes 2359304 | tf_op jit(solution)/shard_map/ppermute | solution.py:97
  33.9 34.7 %collective-permute-start.17 = (bf16[1536,384]{1,0:T(8,128)(2,1)}, bf16[1536,384]{1,0:T(8,128)(2,1)}, u32[]{:S(2)}, u32[]{:S(2)}) collective-permute-start(bf16[1536,384]{1,0:T(8,128)(2,1)} %constant_dynamic-slice_fusion), channel_id=1, source_target_pairs={{0,1},{1,0},{2,3},{3,2},{4,5},{5,4},{6,7},{7,6},{8,9},{9,8},{10,11... | collective-permute-start | bytes 3538952 | tf_op jit(solution)/shard_map/ppermute | solution.py:97
  40.9 24.5 %collective-permute-start.2 = (bf16[1024,384]{1,0:T(8,128)(2,1)}, bf16[1024,384]{1,0:T(8,128)(2,1)S(1)}, u32[]{:S(2)}, u32[]{:S(2)}) collective-permute-start(bf16[1024,384]{1,0:T(8,128)(2,1)} %shard_map.75.refs_0_), channel_id=1, source_target_pairs={{0,4},{1,5},{2,6},{3,7},{4,0},{5,1},{6,2},{7,3},{8,12},{9,13},{10,... | collective-permute-start | bytes 2359304 | tf_op jit(solution)/shard_map/ppermute | solution.py:97
  65.5 43.1 %collective-permute-start.7 = (bf16[1024,384]{1,0:T(8,128)(2,1)}, bf16[1024,384]{1,0:T(8,128)(2,1)}, u32[]{:S(2)}, u32[]{:S(2)}) collective-permute-start(bf16[1024,384]{1,0:T(8,128)(2,1)} %shard_map.77.refs_5_), channel_id=1, source_target_pairs={{0,2},{1,3},{2,0},{3,1},{4,6},{5,7},{6,4},{7,5},{8,10},{9,11},{10,... | collective-permute-start | bytes 2359304 | tf_op jit(solution)/shard_map/ppermute | solution.py:97
  66.1 42.8 %collective-permute-start.8 = (bf16[1024,384]{1,0:T(8,128)(2,1)}, bf16[1024,384]{1,0:T(8,128)(2,1)}, u32[]{:S(2)}, u32[]{:S(2)}) collective-permute-start(bf16[1024,384]{1,0:T(8,128)(2,1)} %shard_map.77.refs_5_), channel_id=1, source_target_pairs={{0,4},{1,5},{2,6},{3,7},{4,0},{5,1},{6,2},{7,3},{8,12},{9,13},{10,... | collective-permute-start | bytes 2359304 | tf_op jit(solution)/shard_map/ppermute | solution.py:97
  68.6 39.2 %collective-permute-start.3 = (bf16[512,384]{1,0:T(8,128)(2,1)}, bf16[512,384]{1,0:T(8,128)(2,1)S(1)}, u32[]{:S(2)}, u32[]{:S(2)}) collective-permute-start(bf16[512,384]{1,0:T(8,128)(2,1)} %get-tuple-element.50), channel_id=1, source_target_pairs={{0,4},{1,5},{2,6},{3,7},{4,0},{5,1},{6,2},{7,3},{8,12},{9,13},{10,... | collective-permute-start | bytes 1179656 | tf_op jit(solution)/shard_map/ppermute | solution.py:97
  81.0 34.9 %collective-permute-start.39 = (bf16[1024,384]{1,0:T(8,128)(2,1)}, bf16[1024,384]{1,0:T(8,128)(2,1)S(1)}, u32[]{:S(2)}, u32[]{:S(2)}) collective-permute-start(bf16[1024,384]{1,0:T(8,128)(2,1)} %shard_map.87.refs_5_), channel_id=1, source_target_pairs={{0,2},{1,3},{2,0},{3,1},{4,6},{5,7},{6,4},{7,5},{8,10},{9,11},{10,... | collective-permute-start | bytes 2359304 | tf_op jit(solution)/shard_map/ppermute | solution.py:97
  82.5 40.0 %collective-permute-start.40 = (bf16[1024,384]{1,0:T(8,128)(2,1)}, bf16[1024,384]{1,0:T(8,128)(2,1)S(1)}, u32[]{:S(2)}, u32[]{:S(2)}) collective-permute-start(bf16[1024,384]{1,0:T(8,128)(2,1)} %shard_map.87.refs_5_), channel_id=1, source_target_pairs={{0,4},{1,5},{2,6},{3,7},{4,0},{5,1},{6,2},{7,3},{8,12},{9,13},{10,... | collective-permute-start | bytes 2359304 | tf_op jit(solution)/shard_map/ppermute | solution.py:97
  107.8 31.0 %collective-permute-start.12 = (bf16[384,768]{1,0:T(8,128)(2,1)}, bf16[384,768]{1,0:T(8,128)(2,1)}, u32[]{:S(2)}, u32[]{:S(2)}) collective-permute-start(bf16[384,768]{1,0:T(8,128)(2,1)} %get-tuple-element.55), channel_id=1, source_target_pairs={{0,8},{1,9},{2,10},{3,11},{4,12},{5,13},{6,14},{7,15},{8,0},{9,1},... | collective-permute-start | bytes 1769480 | tf_op jit(solution)/shard_map/ppermute | solution.py:97
  108.5 42.8 %collective-permute-start.13 = (bf16[384,768]{1,0:T(8,128)(2,1)}, bf16[384,768]{1,0:T(8,128)(2,1)}, u32[]{:S(2)}, u32[]{:S(2)}) collective-permute-start(bf16[384,768]{1,0:T(8,128)(2,1)} %get-tuple-element.56), channel_id=1, source_target_pairs={{0,16},{1,17},{2,18},{3,19},{4,20},{5,21},{6,22},{7,23},{8,24},{9,... | collective-permute-start | bytes 1769480 | tf_op jit(solution)/shard_map/ppermute | solution.py:97
  108.9 43.9 %collective-permute-start.14 = (bf16[384,768]{1,0:T(8,128)(2,1)}, bf16[384,768]{1,0:T(8,128)(2,1)}, u32[]{:S(2)}, u32[]{:S(2)}) collective-permute-start(bf16[384,768]{1,0:T(8,128)(2,1)} %get-tuple-element.57), channel_id=1, source_target_pairs={{0,24},{1,25},{2,26},{3,27},{4,28},{5,29},{6,30},{7,31},{8,16},{9,... | collective-permute-start | bytes 1769480 | tf_op jit(solution)/shard_map/ppermute | solution.py:97
  115.9 54.7 %collective-permute-start.18 = (bf16[768,384]{1,0:T(8,128)(2,1)}, bf16[768,384]{1,0:T(8,128)(2,1)}, u32[]{:S(2)}, u32[]{:S(2)}) collective-permute-start(bf16[768,384]{1,0:T(8,128)(2,1)} %get-tuple-element.60), channel_id=1, source_target_pairs={{0,8},{1,9},{2,10},{3,11},{4,12},{5,13},{6,14},{7,15},{8,0},{9,1},... | collective-permute-start | bytes 1769480 | tf_op jit(solution)/shard_map/ppermute | solution.py:97
  122.5 77.4 %collective-permute-start.19 = (bf16[768,384]{1,0:T(8,128)(2,1)}, bf16[768,384]{1,0:T(8,128)(2,1)}, u32[]{:S(2)}, u32[]{:S(2)}) collective-permute-start(bf16[768,384]{1,0:T(8,128)(2,1)} %get-tuple-element.61), channel_id=1, source_target_pairs={{0,16},{1,17},{2,18},{3,19},{4,20},{5,21},{6,22},{7,23},{8,24},{9,... | collective-permute-start | bytes 1769480 | tf_op jit(solution)/shard_map/ppermute | solution.py:97
  138.7 22.3 %collective-permute-start.4 = (bf16[512,384]{1,0:T(8,128)(2,1)}, bf16[512,384]{1,0:T(8,128)(2,1)S(1)}, u32[]{:S(2)}, u32[]{:S(2)}) collective-permute-start(bf16[512,384]{1,0:T(8,128)(2,1)} %get-tuple-element.51), channel_id=1, source_target_pairs={{0,2},{1,3},{2,0},{3,1},{4,6},{5,7},{6,4},{7,5},{8,10},{9,11},{10,... | collective-permute-start | bytes 1179656 | tf_op jit(solution)/shard_map/ppermute | solution.py:97
  161.1 49.5 %collective-permute-start.20 = (bf16[768,384]{1,0:T(8,128)(2,1)}, bf16[768,384]{1,0:T(8,128)(2,1)}, u32[]{:S(2)}, u32[]{:S(2)}) collective-permute-start(bf16[768,384]{1,0:T(8,128)(2,1)} %get-tuple-element.62), channel_id=1, source_target_pairs={{0,24},{1,25},{2,26},{3,27},{4,28},{5,29},{6,30},{7,31},{8,16},{9,... | collective-permute-start | bytes 1769480 | tf_op jit(solution)/shard_map/ppermute | solution.py:97
  161.8 52.5 %collective-permute-start.35 = (bf16[512,384]{1,0:T(8,128)(2,1)}, bf16[512,384]{1,0:T(8,128)(2,1)S(1)}, u32[]{:S(2)}, u32[]{:S(2)}) collective-permute-start(bf16[512,384]{1,0:T(8,128)(2,1)} %get-tuple-element.73), channel_id=1, source_target_pairs={{0,4},{1,5},{2,6},{3,7},{4,0},{5,1},{6,2},{7,3},{8,12},{9,13},{10,... | collective-permute-start | bytes 1179656 | tf_op jit(solution)/shard_map/ppermute | solution.py:97
  163.3 51.0 %collective-permute-start.36 = (bf16[512,384]{1,0:T(8,128)(2,1)}, bf16[512,384]{1,0:T(8,128)(2,1)}, u32[]{:S(2)}, u32[]{:S(2)}) collective-permute-start(bf16[512,384]{1,0:T(8,128)(2,1)} %get-tuple-element.74), channel_id=1, source_target_pairs={{0,2},{1,3},{2,0},{3,1},{4,6},{5,7},{6,4},{7,5},{8,10},{9,11},{10,... | collective-permute-start | bytes 1179656 | tf_op jit(solution)/shard_map/ppermute | solution.py:97
  170.6 43.7 %collective-permute-start.41 = (bf16[512,384]{1,0:T(8,128)(2,1)}, bf16[512,384]{1,0:T(8,128)(2,1)}, u32[]{:S(2)}, u32[]{:S(2)}) collective-permute-start(bf16[512,384]{1,0:T(8,128)(2,1)} %get-tuple-element.75), channel_id=1, source_target_pairs={{0,4},{1,5},{2,6},{3,7},{4,0},{5,1},{6,2},{7,3},{8,12},{9,13},{10,... | collective-permute-start | bytes 1179656 | tf_op jit(solution)/shard_map/ppermute | solution.py:97
  210.6 22.1 %collective-permute-start.15 = (f32[2048,384]{1,0:T(8,128)S(1)}, f32[2048,384]{1,0:T(8,128)}, u32[]{:S(2)}, u32[]{:S(2)}) collective-permute-start(f32[2048,384]{1,0:T(8,128)S(1)} %slice.185), channel_id=1, source_target_pairs={{0,1},{1,0},{2,3},{3,2},{4,5},{5,4},{6,7},{7,6},{8,9},{9,8},{10,11... | collective-permute-start | bytes 9437192 | tf_op jit(solution)/shard_map/ppermute | solution.py:97
  242.7 32.9 %collective-permute-start.44 = (bf16[2048,384]{1,0:T(8,128)(2,1)}, bf16[2048,384]{1,0:T(8,128)(2,1)}, u32[]{:S(2)}, u32[]{:S(2)}) collective-permute-start(bf16[2048,384]{1,0:T(8,128)(2,1)} %fusion.5), channel_id=1, source_target_pairs={{0,1},{1,0},{2,3},{3,2},{4,5},{5,4},{6,7},{7,6},{8,9},{9,8},{10,11... | collective-permute-start | bytes 4718600 | tf_op jit(solution)/shard_map/ppermute | solution.py:97
  261.8 45.7 %collective-permute-start.27 = (bf16[512,384]{1,0:T(8,128)(2,1)}, bf16[512,384]{1,0:T(8,128)(2,1)}, u32[]{:S(2)}, u32[]{:S(2)}) collective-permute-start(bf16[512,384]{1,0:T(8,128)(2,1)} %get-tuple-element.72), channel_id=1, source_target_pairs={{0,2},{1,3},{2,0},{3,1},{4,6},{5,7},{6,4},{7,5},{8,10},{9,11},{10,... | collective-permute-start | bytes 1179656 | tf_op jit(solution)/shard_map/ppermute | solution.py:97
  262.9 47.3 %collective-permute-start.25 = (bf16[512,384]{1,0:T(8,128)(2,1)}, bf16[512,384]{1,0:T(8,128)(2,1)}, u32[]{:S(2)}, u32[]{:S(2)}) collective-permute-start(bf16[512,384]{1,0:T(8,128)(2,1)} %get-tuple-element.70), channel_id=1, source_target_pairs={{0,4},{1,5},{2,6},{3,7},{4,0},{5,1},{6,2},{7,3},{8,12},{9,13},{10,... | collective-permute-start | bytes 1179656 | tf_op jit(solution)/shard_map/ppermute | solution.py:97
  265.5 46.8 %collective-permute-start.23 = (bf16[512,384]{1,0:T(8,128)(2,1)}, bf16[512,384]{1,0:T(8,128)(2,1)}, u32[]{:S(2)}, u32[]{:S(2)}) collective-permute-start(bf16[512,384]{1,0:T(8,128)(2,1)} %get-tuple-element.67), channel_id=1, source_target_pairs={{0,2},{1,3},{2,0},{3,1},{4,6},{5,7},{6,4},{7,5},{8,10},{9,11},{10,... | collective-permute-start | bytes 1179656 | tf_op jit(solution)/shard_map/ppermute | solution.py:97
  266.1 48.1 %collective-permute-start.21 = (bf16[512,384]{1,0:T(8,128)(2,1)}, bf16[512,384]{1,0:T(8,128)(2,1)}, u32[]{:S(2)}, u32[]{:S(2)}) collective-permute-start(bf16[512,384]{1,0:T(8,128)(2,1)} %get-tuple-element.65), channel_id=1, source_target_pairs={{0,4},{1,5},{2,6},{3,7},{4,0},{5,1},{6,2},{7,3},{8,12},{9,13},{10,... | collective-permute-start | bytes 1179656 | tf_op jit(solution)/shard_map/ppermute | solution.py:97
  319.5 25.4 %collective-permute-start.28 = (bf16[1024,384]{1,0:T(8,128)(2,1)}, bf16[1024,384]{1,0:T(8,128)(2,1)}, u32[]{:S(2)}, u32[]{:S(2)}) collective-permute-start(bf16[1024,384]{1,0:T(8,128)(2,1)} %pad_maximum_fusion.6), channel_id=1, source_target_pairs={{0,4},{1,5},{2,6},{3,7},{4,0},{5,1},{6,2},{7,3},{8,12},{9,13},{10,... | collective-permute-start | bytes 2359304 | tf_op jit(solution)/shard_map/ppermute | solution.py:97
  328.0 33.8 %collective-permute-start.52 = (bf16[1024,384]{1,0:T(8,128)(2,1)}, bf16[1024,384]{1,0:T(8,128)(2,1)}, u32[]{:S(2)}, u32[]{:S(2)}) collective-permute-start(bf16[1024,384]{1,0:T(8,128)(2,1)} %pad_maximum_fusion.10), channel_id=1, source_target_pairs={{0,4},{1,5},{2,6},{3,7},{4,0},{5,1},{6,2},{7,3},{8,12},{9,13},{10,... | collective-permute-start | bytes 2359304 | tf_op jit(solution)/shard_map/ppermute | solution.py:97
  329.7 34.0 %collective-permute-start.50 = (bf16[1024,384]{1,0:T(8,128)(2,1)}, bf16[1024,384]{1,0:T(8,128)(2,1)}, u32[]{:S(2)}, u32[]{:S(2)}) collective-permute-start(bf16[1024,384]{1,0:T(8,128)(2,1)} %pad_maximum_fusion.9), channel_id=1, source_target_pairs={{0,2},{1,3},{2,0},{3,1},{4,6},{5,7},{6,4},{7,5},{8,10},{9,11},{10,... | collective-permute-start | bytes 2359304 | tf_op jit(solution)/shard_map/ppermute | solution.py:97
  336.4 42.1 %collective-permute-start.24 = (bf16[1024,384]{1,0:T(8,128)(2,1)}, bf16[1024,384]{1,0:T(8,128)(2,1)S(1)}, u32[]{:S(2)}, u32[]{:S(2)}) collective-permute-start(bf16[1024,384]{1,0:T(8,128)(2,1)} %pad_maximum_fusion.4), channel_id=1, source_target_pairs={{0,4},{1,5},{2,6},{3,7},{4,0},{5,1},{6,2},{7,3},{8,12},{9,13},{10,... | collective-permute-start | bytes 2359304 | tf_op jit(solution)/shard_map/ppermute | solution.py:97
  344.9 36.2 %collective-permute-start.22 = (bf16[1024,384]{1,0:T(8,128)(2,1)S(1)}, bf16[1024,384]{1,0:T(8,128)(2,1)S(1)}, u32[]{:S(2)}, u32[]{:S(2)}) collective-permute-start(bf16[1024,384]{1,0:T(8,128)(2,1)S(1)} %copy-done.20), channel_id=1, source_target_pairs={{0,2},{1,3},{2,0},{3,1},{4,6},{5,7},{6,4},{7,5},{8,10},{9,11},{10,... | collective-permute-start | bytes 2359304 | tf_op jit(solution)/shard_map/ppermute | solution.py:97
  347.2 46.0 %collective-permute-start.48 = (bf16[1024,384]{1,0:T(8,128)(2,1)S(1)}, bf16[1024,384]{1,0:T(8,128)(2,1)S(1)}, u32[]{:S(2)}, u32[]{:S(2)}) collective-permute-start(bf16[1024,384]{1,0:T(8,128)(2,1)S(1)} %copy-done.22), channel_id=1, source_target_pairs={{0,4},{1,5},{2,6},{3,7},{4,0},{5,1},{6,2},{7,3},{8,12},{9,13},{10,... | collective-permute-start | bytes 2359304 | tf_op jit(solution)/shard_map/ppermute | solution.py:97
  361.8 39.2 %collective-permute-start.46 = (bf16[1024,384]{1,0:T(8,128)(2,1)S(1)}, bf16[1024,384]{1,0:T(8,128)(2,1)S(1)}, u32[]{:S(2)}, u32[]{:S(2)}) collective-permute-start(bf16[1024,384]{1,0:T(8,128)(2,1)S(1)} %copy-done.21), channel_id=1, source_target_pairs={{0,2},{1,3},{2,0},{3,1},{4,6},{5,7},{6,4},{7,5},{8,10},{9,11},{10,... | collective-permute-start | bytes 2359304 | tf_op jit(solution)/shard_map/ppermute | solution.py:97
  363.7 25.3 %collective-permute-start.30 = (bf16[512,384]{1,0:T(8,128)(2,1)S(1)}, bf16[512,384]{1,0:T(8,128)(2,1)S(1)}, u32[]{:S(2)}, u32[]{:S(2)}) collective-permute-start(bf16[512,384]{1,0:T(8,128)(2,1)S(1)} %get-tuple-element.101), channel_id=1, source_target_pairs={{0,8},{1,9},{2,10},{3,11},{4,12},{5,13},{6,14},{7,15},{8,0},{9,1},... | collective-permute-start | bytes 1179656 | tf_op jit(solution)/shard_map/ppermute | solution.py:97
  378.5 32.9 %collective-permute-start.57 = (bf16[768,384]{1,0:T(8,128)(2,1)S(1)}, bf16[768,384]{1,0:T(8,128)(2,1)S(1)}, u32[]{:S(2)}, u32[]{:S(2)}) collective-permute-start(bf16[768,384]{1,0:T(8,128)(2,1)S(1)} %copy-done.49), channel_id=1, source_target_pairs={{0,24},{1,25},{2,26},{3,27},{4,28},{5,29},{6,30},{7,31},{8,16},{9,... | collective-permute-start | bytes 1769480 | tf_op jit(solution)/shard_map/ppermute | solution.py:97
  381.1 30.1 %collective-permute-start.54 = (bf16[512,384]{1,0:T(8,128)(2,1)S(1)}, bf16[512,384]{1,0:T(8,128)(2,1)S(1)}, u32[]{:S(2)}, u32[]{:S(2)}) collective-permute-start(bf16[512,384]{1,0:T(8,128)(2,1)S(1)} %get-tuple-element.99), channel_id=1, source_target_pairs={{0,8},{1,9},{2,10},{3,11},{4,12},{5,13},{6,14},{7,15},{8,0},{9,1},... | collective-permute-start | bytes 1179656 | tf_op jit(solution)/shard_map/ppermute | solution.py:97
  389.7 42.1 %collective-permute-start.61 = (bf16[384,768]{1,0:T(8,128)(2,1)S(1)}, bf16[384,768]{1,0:T(8,128)(2,1)S(1)}, u32[]{:S(2)}, u32[]{:S(2)}) collective-permute-start(bf16[384,768]{1,0:T(8,128)(2,1)S(1)} %copy-done.50), channel_id=1, source_target_pairs={{0,24},{1,25},{2,26},{3,27},{4,28},{5,29},{6,30},{7,31},{8,16},{9,... | collective-permute-start | bytes 1769480 | tf_op jit(solution)/shard_map/ppermute | solution.py:97
  393.2 75.9 %collective-permute-start.58 = (bf16[768,384]{1,0:T(8,128)(2,1)S(1)}, bf16[768,384]{1,0:T(8,128)(2,1)S(1)}, u32[]{:S(2)}, u32[]{:S(2)}) collective-permute-start(bf16[768,384]{1,0:T(8,128)(2,1)S(1)} %copy-done.47), channel_id=1, source_target_pairs={{0,16},{1,17},{2,18},{3,19},{4,20},{5,21},{6,22},{7,23},{8,24},{9,... | collective-permute-start | bytes 1769480 | tf_op jit(solution)/shard_map/ppermute | solution.py:97
  401.0 82.2 %collective-permute-start.59 = (bf16[768,384]{1,0:T(8,128)(2,1)S(1)}, bf16[768,384]{1,0:T(8,128)(2,1)S(1)}, u32[]{:S(2)}, u32[]{:S(2)}) collective-permute-start(bf16[768,384]{1,0:T(8,128)(2,1)S(1)} %copy-done.45), channel_id=1, source_target_pairs={{0,8},{1,9},{2,10},{3,11},{4,12},{5,13},{6,14},{7,15},{8,0},{9,1},... | collective-permute-start | bytes 1769480 | tf_op jit(solution)/shard_map/ppermute | solution.py:97
  411.2 68.9 %collective-permute-start.62 = (bf16[384,768]{1,0:T(8,128)(2,1)S(1)}, bf16[384,768]{1,0:T(8,128)(2,1)S(1)}, u32[]{:S(2)}, u32[]{:S(2)}) collective-permute-start(bf16[384,768]{1,0:T(8,128)(2,1)S(1)} %copy-done.48), channel_id=1, source_target_pairs={{0,16},{1,17},{2,18},{3,19},{4,20},{5,21},{6,22},{7,23},{8,24},{9,... | collective-permute-start | bytes 1769480 | tf_op jit(solution)/shard_map/ppermute | solution.py:97
  411.4 72.8 %collective-permute-start.63 = (bf16[384,768]{1,0:T(8,128)(2,1)S(1)}, bf16[384,768]{1,0:T(8,128)(2,1)S(1)}, u32[]{:S(2)}, u32[]{:S(2)}) collective-permute-start(bf16[384,768]{1,0:T(8,128)(2,1)S(1)} %copy-done.46), channel_id=1, source_target_pairs={{0,8},{1,9},{2,10},{3,11},{4,12},{5,13},{6,14},{7,15},{8,0},{9,1},... | collective-permute-start | bytes 1769480 | tf_op jit(solution)/shard_map/ppermute | solution.py:97
  431.8 73.6 %collective-permute-start.29 = (bf16[512,384]{1,0:T(8,128)(2,1)S(1)}, bf16[512,384]{1,0:T(8,128)(2,1)S(1)}, u32[]{:S(2)}, u32[]{:S(2)}) collective-permute-start(bf16[512,384]{1,0:T(8,128)(2,1)S(1)} %get-tuple-element.100), channel_id=1, source_target_pairs={{0,8},{1,9},{2,10},{3,11},{4,12},{5,13},{6,14},{7,15},{8,0},{9,1},... | collective-permute-start | bytes 1179656 | tf_op jit(solution)/shard_map/ppermute | solution.py:97
  469.1 41.5 %collective-permute-start.53 = (bf16[512,384]{1,0:T(8,128)(2,1)S(1)}, bf16[512,384]{1,0:T(8,128)(2,1)S(1)}, u32[]{:S(2)}, u32[]{:S(2)}) collective-permute-start(bf16[512,384]{1,0:T(8,128)(2,1)S(1)} %get-tuple-element.98), channel_id=1, source_target_pairs={{0,8},{1,9},{2,10},{3,11},{4,12},{5,13},{6,14},{7,15},{8,0},{9,1},... | collective-permute-start | bytes 1179656 | tf_op jit(solution)/shard_map/ppermute | solution.py:97
  480.1 25.3 %collective-permute-start.31 = (bf16[512,384]{1,0:T(8,128)(2,1)S(1)}, bf16[512,384]{1,0:T(8,128)(2,1)S(1)}, u32[]{:S(2)}, u32[]{:S(2)}) collective-permute-start(bf16[512,384]{1,0:T(8,128)(2,1)S(1)} %add_convert_fusion.12), channel_id=1, source_target_pairs={{0,24},{1,25},{2,26},{3,27},{4,28},{5,29},{6,30},{7,31},{8,16},{9,... | collective-permute-start | bytes 1179656 | tf_op jit(solution)/shard_map/ppermute | solution.py:97
  483.2 27.5 %collective-permute-start.55 = (bf16[512,384]{1,0:T(8,128)(2,1)S(1)}, bf16[512,384]{1,0:T(8,128)(2,1)S(1)}, u32[]{:S(2)}, u32[]{:S(2)}) collective-permute-start(bf16[512,384]{1,0:T(8,128)(2,1)S(1)} %add_convert_fusion.1), channel_id=1, source_target_pairs={{0,24},{1,25},{2,26},{3,27},{4,28},{5,29},{6,30},{7,31},{8,16},{9,... | collective-permute-start | bytes 1179656 | tf_op jit(solution)/shard_map/ppermute | solution.py:97
  (72 other events, 954.5 us)
